TPU v7x, 32 devices: a whole 2x2x4 slice. The times are simulated.
32 devices in a mesh: row: 8 (over z, y), col: 4 (over x, core).
Axes of the slice: x: 2, y: 2, z: 4, core: 2. Of those that a mesh axis runs over, the one named last changes fastest.
Arguments:
- start_block: float32 [64, 16, 128], P(('row', 'col')), may hold values from -6 to 6
- blocks: float32 [8, 4, 58, 128, 128], P('row', 'col'), as said below
- slot_row: int32 [8, 4, 58], P('row', 'col'), may hold values from 0 to 7, as said below
- slot_col: int32 [8, 4, 58], P('row', 'col'), may hold values from 0 to 15, as said below
- counts: int32 [8, 4], P('row', 'col'), may hold values from 34 to 58, as said below
Outputs:
- alphas: float32 [2, 16, 16], replicated
- betas: float32 [2, 16, 16], replicated
- next_block: float32 [64, 16, 128], P(('row', 'col'))
Inputs may be any that keep to these rules, and one draw needn't show every extreme that they name: `blocks`: over all cells the live slots list each nonzero block of a symmetric matrix exactly once: block (J, I) is listed exactly when (I, J) is, holding its transpose. Slots at or past a cell's count hold finite values that are no part of H. `counts`: live slots of a cell come first; in every draw some cell has all 58 slots live. `slot_row`: for live slots, the block row within the cell's row group of 8 block rows. `slot_col`: for live slots, the position within the cell's column group of 16 block columns, as in the first step.
All inputs are finite; a program needn't handle non-finite values.
Results may differ from a plain program's by a relative error of at most 0.0003.
Values sent between devices are 32-bit elements; how exact they have to be, the bound alone decides.
A program may use at most 64 MiB of HBM per device.

v0:
```python
import jax
import jax.numpy as jnp
from jax import lax
from jax.sharding import PartitionSpec as P

ITERS = 2


highest = lax.Precision.HIGHEST


def matmul(left, right):
    return jnp.dot(left, right, precision=highest, preferred_element_type=jnp.float32)


def local_gram(left, right):
    return jnp.einsum(
        "bki,bli->kl", left, right, precision=highest, preferred_element_type=jnp.float32
    )


def on_device(start_block, blocks, slot_row, slot_col, counts):
    matrix_tiles = blocks[0, 0]
    rows_local = slot_row[0, 0]
    cols_local = slot_col[0, 0]
    capacity = matrix_tiles.shape[0]
    active = lax.iota(jnp.int32, capacity) < counts[0, 0]
    piece_rows = start_block.shape[0]
    vec_count = start_block.shape[1]
    orbitals = start_block.shape[2]
    row_total = float(piece_rows * lax.axis_size("row") * lax.axis_size("col") * orbitals)
    identity = jnp.eye(vec_count, dtype=jnp.float32)
    start_mean = lax.psum(local_gram(start_block, start_block), ("row", "col")) / row_total
    factor = jnp.linalg.cholesky(start_mean)
    inverse = jax.scipy.linalg.solve_triangular(factor, identity, lower=True)
    vectors = jnp.einsum(
        "kl,bli->bki", inverse, start_block, precision=highest, preferred_element_type=jnp.float32
    )
    previous = jnp.zeros(vectors.shape, jnp.float32)
    beta_prev = jnp.zeros((vec_count, vec_count), jnp.float32)
    alpha_list = []
    beta_list = []
    for iteration in range(ITERS):
        gathered = lax.all_gather(vectors, "row", axis=0, tiled=True)
        operate_product = jnp.einsum(
            "sij,skj->ski",
            matrix_tiles,
            gathered[cols_local],
            precision=highest,
            preferred_element_type=jnp.float32,
        )
        targets = lax.iota(jnp.int32, lax.axis_size("col") * piece_rows)
        selector = ((rows_local[None, :] == targets[:, None]) & active[None, :]).astype(jnp.float32)
        image_block = lax.psum_scatter(
            jnp.einsum(
                "rs,ski->rki",
                selector,
                operate_product,
                precision=highest,
                preferred_element_type=jnp.float32,
            ),
            "col",
            scatter_dimension=0,
            tiled=True,
        )
        stacked = jnp.concatenate([image_block, vectors, previous], axis=1)
        all_means = lax.psum(local_gram(stacked, stacked), ("row", "col")) / row_total
        yy_mean = all_means[:vec_count, :vec_count]
        vy_mean = all_means[vec_count : 2 * vec_count, :vec_count]
        py_mean = all_means[2 * vec_count :, :vec_count]
        vv_mean = all_means[vec_count : 2 * vec_count, vec_count : 2 * vec_count]
        pv_mean = all_means[2 * vec_count :, vec_count : 2 * vec_count]
        pp_mean = all_means[2 * vec_count :, 2 * vec_count :]
        residual = image_block - jnp.einsum(
            "lk,bli->bki", vy_mean, vectors, precision=highest, preferred_element_type=jnp.float32
        )
        residual = residual - jnp.einsum(
            "kl,bli->bki",
            beta_prev,
            previous,
            precision=highest,
            preferred_element_type=jnp.float32,
        )
        gram_mean = yy_mean - matmul(vy_mean.T, vy_mean) - matmul(vy_mean.T, vy_mean)
        gram_mean = gram_mean + matmul(matmul(vy_mean.T, vv_mean), vy_mean)
        gram_mean = gram_mean - matmul(py_mean.T, beta_prev.T) - matmul(beta_prev, py_mean)
        gram_mean = gram_mean + matmul(matmul(vy_mean.T, pv_mean.T), beta_prev.T)
        gram_mean = gram_mean + matmul(matmul(beta_prev, pv_mean), vy_mean)
        gram_mean = gram_mean + matmul(matmul(beta_prev, pp_mean), beta_prev.T)
        factor = jnp.linalg.cholesky(gram_mean)
        beta_block = factor.T
        inverse = jax.scipy.linalg.solve_triangular(factor, identity, lower=True)
        previous = vectors
        vectors = jnp.einsum(
            "kl,bli->bki", inverse, residual, precision=highest, preferred_element_type=jnp.float32
        )
        beta_prev = beta_block
        alpha_list.append(vy_mean)
        beta_list.append(beta_block)
    return (jnp.stack(alpha_list), jnp.stack(beta_list), vectors)


def solution(mesh):
    placed = (
        P(("row", "col"), None, None),
        P("row", "col", None, None, None),
        P("row", "col", None),
        P("row", "col", None),
        P("row", "col"),
    )
    return jax.shard_map(
        on_device,
        mesh=mesh,
        in_specs=placed,
        out_specs=(P(), P(), P(("row", "col"), None, None)),
        check_vma=False,
    )
```

profile of v0, /device:TPU:0, one launch (start us, length us, event | category | flops | bytes accessed | tf_op | source)
XLA Modules:
  0.0 285.7 jit_solution(17474431526224107313)
XLA Ops:
  7.9 0.7 fusion.84
  8.7 42.0 %psum.21 = f32[16,16]{0,1:T(8,128)S(1)} all-reduce(f32[16,16]{0,1:T(8,128)S(1)} %convolution_bitcast_fusion.12), channel_id=1, replica_groups=mesh['row'=8,'col'=4] {'row','col'}, use_global_device_ids=true, to_apply=%region_0.0 | all-reduce | flops 256 | bytes 2048 | tf_op jit(solution)/shard_map/psum | solution.py:33
  50.8 1.5 cholesky.59
  52.9 0.6 fusion.25
  53.6 1.2 custom-call.7
  55.1 30.6 %all_gather.6 = f32[16,16,128]{2,1,0:T(8,128)S(1)} all-gather(f32[2,16,128]{2,1,0:T(8,128)S(1)} %convolution_bitcast_fusion.8), channel_id=1, replica_groups=mesh['row'=8,'col'=4] {'row'}, dimensions={0}, use_global_device_ids=true | all-gather | bytes 147456 | tf_op jit(solution)/shard_map/all_gather | solution.py:44
  86.4 8.1 %fusion.2 = f32[58,16,128]{2,1,0:T(8,128)S(1)} fusion(f32[58,16,128]{2,1,0:T(8,128)S(1)} %gather_fusion, f32[1,1,58,128,128]{4,3,2,1,0:T(8,128)} %param.9), kind=kOutput, calls=%fused_computation.4 | convolution fusion | flops 182452224 | bytes 4751360 | tf_op jit(solution)/shard_map/sij,skj->ski/dot_general | solution.py:45
  95.6 19.3 %reduce-scatter.3.cloned.1.call-done = f32[2,16,128]{2,1,0:T(8,128)} async-done(((f32[8,16,128]{2,1,0:T(8,128)}), f32[2,16,128]{2,1,0:T(8,128)}) %reduce-scatter.3.cloned.1.call-update) | async-done | bytes 16400 | tf_op jit(solution)/shard_map/reduce_scatter | solution.py:54
  114.9 1.0 convolution_bitcast_fusion.1
  115.9 39.5 %psum.22 = f32[48,48]{0,1:T(8,128)S(1)} all-reduce(f32[48,48]{0,1:T(8,128)S(1)} %convolution_bitcast_fusion.1), channel_id=1, replica_groups=mesh['row'=8,'col'=4] {'row','col'}, use_global_device_ids=true, to_apply=%region_4.0 | all-reduce | flops 2304 | bytes 18432 | tf_op jit(solution)/shard_map/psum | solution.py:67
  156.4 0.9 fusion.7
  158.7 1.5 cholesky.70
  160.8 0.6 fusion.94
  161.5 1.2 custom-call.8
  163.0 30.7 %all_gather.7 = f32[16,16,128]{2,1,0:T(8,128)S(1)} all-gather(f32[2,16,128]{2,1,0:T(8,128)S(1)} %convolution_bitcast_fusion.5), channel_id=1, replica_groups=mesh['row'=8,'col'=4] {'row'}, dimensions={0}, use_global_device_ids=true | all-gather | bytes 147456 | tf_op jit(solution)/shard_map/all_gather | solution.py:44
  194.4 8.1 %fusion = f32[58,16,128]{2,1,0:T(8,128)S(1)} fusion(f32[58,16,128]{2,1,0:T(8,128)S(1)} %gather_fusion.1, f32[1,1,58,128,128]{4,3,2,1,0:T(8,128)} %param.9), kind=kOutput, calls=%fused_computation.2 | convolution fusion | flops 182452224 | bytes 4751360 | tf_op jit(solution)/shard_map/sij,skj->ski/dot_general | solution.py:45
  203.6 20.4 %reduce-scatter.5.cloned.1.call-done = f32[2,16,128]{2,1,0:T(8,128)} async-done(((f32[8,16,128]{2,1,0:T(8,128)}), f32[2,16,128]{2,1,0:T(8,128)}) %reduce-scatter.5.cloned.1.call-update) | async-done | bytes 16400 | tf_op jit(solution)/shard_map/reduce_scatter | solution.py:54
  223.9 1.0 convolution_bitcast_fusion
  224.9 39.5 %psum.23 = f32[48,48]{0,1:T(8,128)S(1)} all-reduce(f32[48,48]{0,1:T(8,128)S(1)} %convolution_bitcast_fusion), channel_id=1, replica_groups=mesh['row'=8,'col'=4] {'row','col'}, use_global_device_ids=true, to_apply=%region_6.9 | all-reduce | flops 2304 | bytes 18432 | tf_op jit(solution)/shard_map/psum | solution.py:67
  264.4 0.8 fusion.44
  265.3 0.9 fusion.26
  266.9 0.9 fusion.5
  267.8 0.8 fusion.4
  268.8 0.9 convolution_subtract_fusion.1
  269.7 0.9 convolution_subtract_fusion
  270.6 0.7 copy.58
  271.2 0.8 convolution_add_fusion.2
  272.3 0.9 convolution_add_fusion
  273.2 1.5 cholesky.81
  276.0 1.2 custom-call.9
  277.5 0.7 copy.59
  278.2 0.7 convolution_bitcast_fusion.2
  (60 shorter events, 10.9 us)
Async XLA Ops:
  7.2 1.4 copy-start
  7.2 87.3 %copy-start.1 = (s32[1,1,58]{2,1,0:T(1,128)S(1)}, s32[1,1,58]{2,1,0:T(1,128)}, u32[]{:S(2)}) copy-start(s32[1,1,58]{2,1,0:T(1,128)} %param.10) | copy-start | bytes 700
  7.2 107.7 %reduce-scatter.3.cloned.1.call-start = ((), (), s32[]{:S(2)}) async-start(), calls=%async_computation.2 | async-start | bytes 81920 | tf_op jit(solution)/shard_map/reduce_scatter | solution.py:54
  95.5 128.4 %reduce-scatter.5.cloned.1.call-start = ((), (), s32[]{:S(2)}) async-start(), calls=%async_computation.3 | async-start | bytes 81920 | tf_op jit(solution)/shard_map/reduce_scatter | solution.py:54
Sparse Core Ops, SparseCore 0:
  95.6 19.2 reduce-scatter.2
  203.6 20.2 reduce-scatter.4
where the time goes:
time: 287 us; the launch traced here: 286 us
  blocking collectives  182 us (63%)
  waiting for transfers between devices  39.7 us (14%)
  matrix products  31.8 us (11%)
  between operations  14.8 us (5%)
  other arithmetic  12.8 us (4%)
  local copies, waits for them, and re-layouts  4.25 us (1%)
    psum x2, blocking collectives, on_device(): lax.psum(local_gram(stacked, stacked), ('row', 'col')) / row_total  79 us
    all_gather x2, blocking collectives, on_device(): gathered = lax.all_gather(vectors, 'row', axis=0, tiled=True)  61.3 us
    psum x1, blocking collectives, on_device(): lax.psum(local_gram(start_block, start_block), ('row', 'col')) / row_total  42 us
    reduce_scatter x2, waiting for transfers between devices, on_device(): lax.psum_scatter(jnp.einsum('rs,ski->rki', selector, operate_product, pre...  39.7 us
    dot_general x2, matrix products, on_device(): jnp.einsum('sij,skj->ski', matrix_tiles, gathered[cols_local], precision=...  16.1 us
    dot_general x22, matrix products, matmul(): jnp.dot(left, right, precision=highest, preferred_element_type=jnp.float32)  8.28 us
  transfers between devices with their start and end apart: 2, of which 2 were waited for; matrix products, arithmetic and copies ran while one was open for 0% of the time, Pallas kernels for 0%

commit v1 on v0

v1 whole, which is shorter than its diff:
```python
import functools

import jax
import jax.numpy as jnp
from jax import lax
from jax.experimental import pallas as pl
from jax.experimental.pallas import tpu as pltpu
from jax.sharding import PartitionSpec as P

HIGHEST = lax.Precision.HIGHEST
F32 = jnp.float32
BF16 = jnp.bfloat16
NN = (((1,), (0,)), ((), ()))
NT = (((1,), (1,)), ((), ()))
TN = (((0,), (0,)), ((), ()))


def dot(left, right, dims=NN):
    return lax.dot_general(left, right, dims, precision=HIGHEST, preferred_element_type=F32)


def factor(gram):
    n = gram.shape[0]
    rows = lax.broadcasted_iota(jnp.int32, (n, n), 0)
    cols = lax.broadcasted_iota(jnp.int32, (n, n), 1)
    work = jnp.concatenate([gram, (rows == cols).astype(F32)], axis=1)
    index = lax.broadcasted_iota(jnp.int32, (n, 2 * n), 0)
    for j in range(n - 1):
        ratio = work[j : j + 1, :] / work[j : j + 1, j : j + 1]
        work = work - jnp.where(index > j, work[:, j : j + 1], 0.0) * ratio
    upper = work[:, :n]
    pivots = jnp.sum(jnp.where(rows == cols, upper, 0.0), axis=1, keepdims=True)
    scale = 1.0 / jnp.sqrt(pivots)
    return jnp.where(rows <= cols, upper, 0.0) * scale, work[:, n:] * scale


def pack(gram):
    quarter = gram.shape[0] // 4
    return jnp.concatenate([gram[i * quarter : (i + 1) * quarter] for i in range(4)], axis=1)


def unpack(packed):
    width = packed.shape[1] // 4
    return jnp.concatenate([packed[:, i * width : (i + 1) * width] for i in range(4)], axis=0)


def kernel(
    nr, nc, group, total,
    rows_ref, cols_ref, counts_ref, start_ref, blocks_ref,
    alphas_ref, betas_ref, next_ref,
    tiles, weights, expanded, gat, xhi, xlo, part, scat, ybuf, gsend, grow, gcol_send, gcol,
    load_sem, row_send, row_recv, col_send, col_recv, gr_send, gr_recv, gc_send, gc_recv,
):
    me_r = lax.axis_index("row")
    me_c = lax.axis_index("col")
    capacity = tiles.shape[0]
    piece, k, orb = start_ref.shape
    local_rows = nc * piece
    count = counts_ref[0]

    load = pltpu.make_async_copy(blocks_ref, tiles, load_sem)
    load.start()

    def row_peer(d):
        return (lax.rem(me_r + d, nr), me_c)

    def col_peer(d):
        return (me_r, lax.rem(me_c + d, nc))

    barrier = pltpu.get_barrier_semaphore()
    for d in range(1, nr):
        pl.semaphore_signal(barrier, inc=1, device_id=row_peer(d), device_id_type=pl.DeviceIdType.MESH)
    for d in range(1, nc):
        pl.semaphore_signal(barrier, inc=1, device_id=col_peer(d), device_id_type=pl.DeviceIdType.MESH)
    pl.semaphore_wait(barrier, nr + nc - 2)

    def spread_row(src, dst, send, recv, step):
        copies = []
        for d in range(1, nr):
            copy = pltpu.make_async_remote_copy(
                src_ref=src, dst_ref=dst.at[me_r],
                send_sem=send.at[step, d], recv_sem=recv.at[step, d],
                device_id=row_peer(d), device_id_type=pl.DeviceIdType.MESH,
            )
            copy.start()
            copies.append(copy)
        return copies

    def spread_col(src, dst, send, recv, step, scatter):
        copies = []
        for d in range(1, nc):
            peer = lax.rem(me_c + d, nc)
            copy = pltpu.make_async_remote_copy(
                src_ref=src.at[peer] if scatter else src, dst_ref=dst.at[me_c],
                send_sem=send.at[step, d], recv_sem=recv.at[step, d],
                device_id=(me_r, peer), device_id_type=pl.DeviceIdType.MESH,
            )
            copy.start()
            copies.append(copy)
        return copies

    def received(copies):
        for copy in copies:
            copy.wait_recv()

    def cat(value):
        return jnp.concatenate([value[p] for p in range(piece)], axis=1)

    pending = []
    first = spread_row(start_ref, gat.at[0], row_send, row_recv, 0)
    pending += first
    gat[0, pl.ds(me_r, 1)] = start_ref[...][None]

    load.wait()

    def split_tile(s, carry):
        tile = lax.select(jnp.broadcast_to(s < count, (orb, orb)), tiles[s], jnp.zeros((orb, orb), F32))
        high = tile.astype(BF16)
        weights[s, :orb] = high
        weights[s, orb:] = (tile - high.astype(F32)).astype(BF16)
        return carry

    lax.fori_loop(0, capacity, split_tile, 0, unroll=2)

    half = local_rows * k

    def operate(step):
        def split_vectors(q, carry):
            for p in range(piece):
                value = gat[step, q, p]
                high = value.astype(BF16)
                xhi[q * piece + p] = high
                xlo[q * piece + p] = (value - high.astype(F32)).astype(BF16)
            return carry

        lax.fori_loop(0, nr, split_vectors, 0, unroll=nr <= 8)

        def chunk(base):
            for t in range(group):
                s = base + t
                col = jnp.clip(lax.select(s < count, cols_ref[s], 0), 0, nr * piece - 1)
                row = rows_ref[s]
                high, low = xhi[col], xlo[col]
                zero = jnp.zeros_like(high)
                for r in range(local_rows):
                    hit = row == r
                    expanded[r * k : (r + 1) * k, t * orb : (t + 1) * orb] = lax.select(hit, high, zero)
                    expanded[half + r * k : half + (r + 1) * k, t * orb : (t + 1) * orb] = lax.select(hit, low, zero)
            flat = jnp.concatenate([weights[base + t] for t in range(group)], axis=1)
            return lax.dot_general(expanded[...], flat, NT, preferred_element_type=F32)

        if capacity == group:
            acc = chunk(0)
        else:
            acc = lax.fori_loop(
                0, capacity // group, lambda g, a: a + chunk(g * group),
                jnp.zeros((2 * half, 2 * orb), F32),
            )
        out = acc[:half, :orb] + acc[:half, orb:] + acc[half:, :orb]
        for r in range(local_rows):
            part[step, r // piece, r % piece] = out[r * k : (r + 1) * k]
        return spread_col(part.at[step], scat.at[step], col_send, col_recv, step, True)

    def reduced(step, copies):
        received(copies)
        own = part[step, me_c]
        for d in range(1, nc):
            own = own + scat[step, lax.rem(me_c + d, nc)]
        return own

    def mean_start(step, gram):
        gsend[step] = pack(gram) * (1.0 / total)
        return spread_row(gsend.at[step], grow.at[step], gr_send, gr_recv, step)

    def mean_middle(step, copies):
        received(copies)
        grow[step, pl.ds(me_r, 1)] = gsend[step][None]
        value = grow[step, 0]
        for r in range(1, nr):
            value = value + grow[step, r]
        gcol_send[step] = value
        return spread_col(gcol_send.at[step], gcol.at[step], gc_send, gc_recv, step, False)

    def mean_end(step, copies):
        received(copies)
        gcol[step, pl.ds(me_c, 1)] = gcol_send[step][None]
        value = gcol[step, 0]
        for c in range(1, nc):
            value = value + gcol[step, c]
        return unpack(value)

    received(first)
    scatter0 = operate(0)
    pending += scatter0
    y_raw = reduced(0, scatter0)
    ybuf[...] = y_raw
    gat[1, pl.ds(me_r, 1)] = y_raw[None]
    second = spread_row(ybuf, gat.at[1], row_send, row_recv, 1)
    pending += second
    s_cat = cat(start_ref)
    y_cat = cat(y_raw)
    both = jnp.concatenate([s_cat, y_cat], axis=0)
    mean0 = mean_start(0, dot(both, both, NT))
    pending += mean0
    received(second)
    middle0 = mean_middle(0, mean0)
    pending += middle0
    scatter1 = operate(1)
    pending += scatter1
    gram = mean_end(0, middle0)
    ss, sy, yy = gram[:k, :k], gram[:k, k:], gram[k:, k:]
    _, inv0 = factor(ss)
    alpha1 = dot(dot(inv0, sy), inv0, NT)
    q1 = dot(dot(inv0, ss), inv0, NT)
    yy1 = dot(dot(inv0, yy), inv0, NT)
    beta1, inv1 = factor(yy1 - dot(alpha1, alpha1, TN) - dot(alpha1, alpha1 - dot(q1, alpha1), TN))
    v1 = dot(inv0, s_cat)
    hv1 = dot(inv0, y_cat)
    v2 = dot(inv1, hv1 - dot(alpha1, v1, TN))
    known = dot(beta1, v1)
    shift = dot(dot(inv1, alpha1, NT), hv1)
    lead = dot(inv1, inv0)
    y2 = dot(lead, cat(reduced(1, scatter1))) - shift
    w2 = y2 - known
    both = jnp.concatenate([v2, w2], axis=0)
    grams = dot(both, jnp.concatenate([both, y2], axis=0), NT)
    top = grams[:k, : 2 * k]
    low = jnp.concatenate([grams[:k, 2 * k :], grams[k:, k : 2 * k]], axis=1)
    mean1 = mean_start(1, jnp.concatenate([top, low], axis=0))
    pending += mean1
    middle1 = mean_middle(1, mean1)
    pending += middle1
    gram = mean_end(1, middle1)
    qq, pw, alpha2, ww = gram[:k, :k], gram[:k, k:], gram[k:, :k], gram[k:, k:]
    rest = pw - dot(qq, alpha2)
    beta2, inv2 = factor(ww - dot(pw, alpha2, TN) - dot(alpha2, rest, TN))
    out = dot(inv2, w2 - dot(alpha2, v2, TN))
    for p in range(piece):
        next_ref[p] = out[:, p * orb : (p + 1) * orb]
    alphas_ref[0] = alpha1
    alphas_ref[1] = alpha2
    betas_ref[0] = beta1
    betas_ref[1] = beta2
    for copy in pending:
        copy.wait_send()


def on_device(nr, nc, start_block, blocks, slot_row, slot_col, counts):
    capacity = blocks.shape[2]
    orb = blocks.shape[3]
    piece, k, _ = start_block.shape
    local_rows = nc * piece
    total = float(piece * nr * nc * orb)
    group = max(g for g in range(1, 65) if capacity % g == 0 and g * local_rows * k <= 64 * 128)
    vmem = pl.BlockSpec(memory_space=pltpu.VMEM)
    smem = pl.BlockSpec(memory_space=pltpu.SMEM)
    dma = pltpu.SemaphoreType.DMA
    width = 4 * 2 * k
    height = 2 * k // 4
    return pl.pallas_call(
        functools.partial(kernel, nr, nc, group, total),
        out_shape=(
            jax.ShapeDtypeStruct((2, k, k), F32),
            jax.ShapeDtypeStruct((2, k, k), F32),
            jax.ShapeDtypeStruct((piece, k, orb), F32),
        ),
        in_specs=[smem, smem, smem, vmem, pl.BlockSpec(memory_space=pl.ANY)],
        out_specs=(vmem, vmem, vmem),
        scratch_shapes=[
            pltpu.VMEM((capacity, orb, orb), F32),
            pltpu.VMEM((capacity, 2 * orb, orb), BF16),
            pltpu.VMEM((2 * local_rows * k, group * orb), BF16),
            pltpu.VMEM((2, nr, piece, k, orb), F32),
            pltpu.VMEM((nr * piece, k, orb), BF16),
            pltpu.VMEM((nr * piece, k, orb), BF16),
            pltpu.VMEM((2, nc, piece, k, orb), F32),
            pltpu.VMEM((2, nc, piece, k, orb), F32),
            pltpu.VMEM((piece, k, orb), F32),
            pltpu.VMEM((2, height, width), F32),
            pltpu.VMEM((2, nr, height, width), F32),
            pltpu.VMEM((2, height, width), F32),
            pltpu.VMEM((2, nc, height, width), F32),
            dma,
            dma((2, nr)), dma((2, nr)),
            dma((2, nc)), dma((2, nc)),
            dma((2, nr)), dma((2, nr)),
            dma((2, nc)), dma((2, nc)),
        ],
        compiler_params=pltpu.CompilerParams(
            collective_id=0, has_side_effects=True, vmem_limit_bytes=60 * 1024 * 1024
        ),
    )(slot_row[0, 0], slot_col[0, 0], counts[0], start_block, blocks[0, 0])


def solution(mesh):
    placed = (
        P(("row", "col"), None, None),
        P("row", "col", None, None, None),
        P("row", "col", None),
        P("row", "col", None),
        P("row", "col"),
    )
    return jax.shard_map(
        functools.partial(on_device, mesh.shape["row"], mesh.shape["col"]),
        mesh=mesh,
        in_specs=placed,
        out_specs=(P(), P(), P(("row", "col"), None, None)),
        check_vma=False,
    )
```

time: 287 us -> 45 us (0.16)
  blocking collectives: 182 us -> 0 us
  waiting for transfers between devices: 39.7 us -> 0 us
  Pallas kernels: 0 us -> 39.2 us
  matrix products: 31.8 us -> 0 us
  between operations: 14.8 us -> 1.29 us
  other arithmetic: 12.8 us -> 0 us
    psum x3 -> x0, blocking collectives: 121 us -> none  [the longest x2 79 us: on_device(): lax.psum(local_gram(stacked, stacked), ('row', 'col')) / row_total]
    all_gather x2 -> x0, blocking collectives: 61.3 us -> none  [on_device(): gathered = lax.all_gather(vectors, 'row', axis=0, tiled=True)]
    reduce_scatter x2 -> x0, waiting for transfers between devices: 39.7 us -> none  [on_device(): lax.psum_scatter(jnp.einsum('rs,ski->rki', selector, operate_product, pre...]
    pallas_call x0 -> x1, Pallas kernels: none -> 39.2 us  [on_device(): pl.pallas_call(functools.partial(kernel, nr, nc, group, total), out_shape...]
    dot_general x36 -> x0, matrix products: 31.2 us -> none  [the longest x2 16.1 us: on_device(): jnp.einsum('sij,skj->ski', matrix_tiles, gathered[cols_local], precision=...]
    another operation x17 -> x0, other arithmetic: 12.1 us -> none  [the longest x5 4.98 us: on_device(): inverse = jax.scipy.linalg.solve_triangular(factor, identity, lower=True)]
  transfers between devices with their start and end apart: 2 -> 0, of which waited for: 2 -> 0; matrix products, arithmetic and copies ran while one was open for 0% -> 0% of each run, Pallas kernels for 0% -> 0%
where the time goes in v1:
time: 45 us; the launch traced here: 44.4 us
  Pallas kernels  39.2 us (87%)
  local copies, waits for them, and re-layouts  3.97 us (9%)
  between operations  1.29 us (3%)
    pallas_call x1, Pallas kernels, on_device(): pl.pallas_call(functools.partial(kernel, nr, nc, group, total), out_shape...  39.2 us
    unnamed x3, local copies, waits for them, and re-layouts  3.97 us

profile of v1, /device:TPU:0, one launch (start us, length us, event | category | flops | bytes accessed | tf_op | source)
XLA Modules:
  0.0 44.4 jit_solution(9348664990969696794)
XLA Ops:
  1.3 39.2 %shard_map.76 = (f32[2,16,16]{2,1,0:T(8,128)}, f32[2,16,16]{2,1,0:T(8,128)}, f32[2,16,128]{2,1,0:T(8,128)}) custom-call(s32[58]{0:T(128)} %bitcast.6, s32[58]{0:T(128)} %bitcast.7, s32[1]{0:T(128)} %bitcast.4.counts_ref, f32[2,16,128]{2,1,0:T(8,128)} %start_ref.1, f32[58,128,128]{2,1,0:T(8,128)} %bitcast.5), custom_call_target="tpu_custom_call" | custom-call | tf_op jit(solution)/shard_map/pallas_call | solution.py:260
  40.5 1.3 %copy.12 = f32[2,16,16]{2,1,0:T(8,128)} copy(f32[2,16,16]{2,1,0:T(8,128)} %get-tuple-element.6) | data formatting | bytes 4096
  41.8 1.3 %copy.13 = f32[2,16,16]{2,1,0:T(8,128)} copy(f32[2,16,16]{2,1,0:T(8,128)} %get-tuple-element.7) | data formatting | bytes 4096
  43.1 1.3 %copy.14 = f32[2,16,128]{2,1,0:T(8,128)} copy(f32[2,16,128]{2,1,0:T(8,128)} %get-tuple-element.8) | data formatting | bytes 32768

commit v2 on v1

--- a/solution.py
+++ b/solution.py
@@ -46,9 +46,10 @@
 
 def kernel(
     nr, nc, group, total,
-    rows_ref, cols_ref, counts_ref, start_ref, blocks_ref,
-    alphas_ref, betas_ref, next_ref,
+    rows_hbm, cols_hbm, counts_hbm, start_ref, blocks_ref,
+    packed_ref,
     tiles, weights, expanded, gat, xhi, xlo, part, scat, ybuf, gsend, grow, gcol_send, gcol,
+    rows_ref, cols_ref, counts_ref,
     load_sem, row_send, row_recv, col_send, col_recv, gr_send, gr_recv, gc_send, gc_recv,
 ):
     me_r = lax.axis_index("row")
@@ -56,10 +57,14 @@
     capacity = tiles.shape[0]
     piece, k, orb = start_ref.shape
     local_rows = nc * piece
-    count = counts_ref[0]
-
-    load = pltpu.make_async_copy(blocks_ref, tiles, load_sem)
-    load.start()
+
+    loads = [
+        pltpu.make_async_copy(start_ref, gat.at[0, me_r], load_sem.at[0]),
+        pltpu.make_async_copy(rows_hbm, rows_ref, load_sem.at[1]),
+        pltpu.make_async_copy(cols_hbm, cols_ref, load_sem.at[2]),
+        pltpu.make_async_copy(counts_hbm, counts_ref, load_sem.at[3]),
+        pltpu.make_async_copy(blocks_ref, tiles, load_sem.at[4]),
+    ]
 
     def row_peer(d):
         return (lax.rem(me_r + d, nr), me_c)
@@ -72,6 +77,8 @@
         pl.semaphore_signal(barrier, inc=1, device_id=row_peer(d), device_id_type=pl.DeviceIdType.MESH)
     for d in range(1, nc):
         pl.semaphore_signal(barrier, inc=1, device_id=col_peer(d), device_id_type=pl.DeviceIdType.MESH)
+    for load in loads:
+        load.start()
     pl.semaphore_wait(barrier, nr + nc - 2)
 
     def spread_row(src, dst, send, recv, step):
@@ -109,9 +116,36 @@
     pending = []
     first = spread_row(start_ref, gat.at[0], row_send, row_recv, 0)
     pending += first
-    gat[0, pl.ds(me_r, 1)] = start_ref[...][None]
-
-    load.wait()
+    def mean_start(step, gram):
+        gsend[step] = pack(gram) * (1.0 / total)
+        return spread_row(gsend.at[step], grow.at[step], gr_send, gr_recv, step)
+
+    def mean_middle(step, copies):
+        received(copies)
+        grow[step, pl.ds(me_r, 1)] = gsend[step][None]
+        value = grow[step, 0]
+        for r in range(1, nr):
+            value = value + grow[step, r]
+        gcol_send[step] = value
+        return spread_col(gcol_send.at[step], gcol.at[step], gc_send, gc_recv, step, False)
+
+    def mean_end(step, copies):
+        received(copies)
+        gcol[step, pl.ds(me_c, 1)] = gcol_send[step][None]
+        value = gcol[step, 0]
+        for c in range(1, nc):
+            value = value + gcol[step, c]
+        return unpack(value)
+
+    loads[0].wait()
+    s_cat = cat(gat[0, me_r])
+    ss = dot(s_cat, s_cat, NT)
+    ss = jnp.concatenate([ss, ss], axis=1)
+    mean_s = mean_start(0, jnp.concatenate([ss, ss], axis=0))
+    pending += mean_s
+    for load in loads[1:]:
+        load.wait()
+    count = counts_ref[0, 0]
 
     def split_tile(s, carry):
         tile = lax.select(jnp.broadcast_to(s < count, (orb, orb)), tiles[s], jnp.zeros((orb, orb), F32))
@@ -168,54 +202,30 @@
             own = own + scat[step, lax.rem(me_c + d, nc)]
         return own
 
-    def mean_start(step, gram):
-        gsend[step] = pack(gram) * (1.0 / total)
-        return spread_row(gsend.at[step], grow.at[step], gr_send, gr_recv, step)
-
-    def mean_middle(step, copies):
-        received(copies)
-        grow[step, pl.ds(me_r, 1)] = gsend[step][None]
-        value = grow[step, 0]
-        for r in range(1, nr):
-            value = value + grow[step, r]
-        gcol_send[step] = value
-        return spread_col(gcol_send.at[step], gcol.at[step], gc_send, gc_recv, step, False)
-
-    def mean_end(step, copies):
-        received(copies)
-        gcol[step, pl.ds(me_c, 1)] = gcol_send[step][None]
-        value = gcol[step, 0]
-        for c in range(1, nc):
-            value = value + gcol[step, c]
-        return unpack(value)
-
     received(first)
+    middle_s = mean_middle(0, mean_s)
+    pending += middle_s
     scatter0 = operate(0)
     pending += scatter0
+    _, inv0 = factor(mean_end(0, middle_s)[:k, :k])
+    v1 = dot(inv0, s_cat)
     y_raw = reduced(0, scatter0)
     ybuf[...] = y_raw
     gat[1, pl.ds(me_r, 1)] = y_raw[None]
     second = spread_row(ybuf, gat.at[1], row_send, row_recv, 1)
     pending += second
-    s_cat = cat(start_ref)
-    y_cat = cat(y_raw)
-    both = jnp.concatenate([s_cat, y_cat], axis=0)
-    mean0 = mean_start(0, dot(both, both, NT))
+    hv1 = dot(inv0, cat(y_raw))
+    both = jnp.concatenate([v1, hv1], axis=0)
+    mean0 = mean_start(1, dot(both, both, NT))
     pending += mean0
     received(second)
-    middle0 = mean_middle(0, mean0)
+    middle0 = mean_middle(1, mean0)
     pending += middle0
     scatter1 = operate(1)
     pending += scatter1
-    gram = mean_end(0, middle0)
-    ss, sy, yy = gram[:k, :k], gram[:k, k:], gram[k:, k:]
-    _, inv0 = factor(ss)
-    alpha1 = dot(dot(inv0, sy), inv0, NT)
-    q1 = dot(dot(inv0, ss), inv0, NT)
-    yy1 = dot(dot(inv0, yy), inv0, NT)
+    gram = mean_end(1, middle0)
+    q1, alpha1, yy1 = gram[:k, :k], gram[:k, k:], gram[k:, k:]
     beta1, inv1 = factor(yy1 - dot(alpha1, alpha1, TN) - dot(alpha1, alpha1 - dot(q1, alpha1), TN))
-    v1 = dot(inv0, s_cat)
-    hv1 = dot(inv0, y_cat)
     v2 = dot(inv1, hv1 - dot(alpha1, v1, TN))
     known = dot(beta1, v1)
     shift = dot(dot(inv1, alpha1, NT), hv1)
@@ -226,23 +236,29 @@
     grams = dot(both, jnp.concatenate([both, y2], axis=0), NT)
     top = grams[:k, : 2 * k]
     low = jnp.concatenate([grams[:k, 2 * k :], grams[k:, k : 2 * k]], axis=1)
-    mean1 = mean_start(1, jnp.concatenate([top, low], axis=0))
+    mean1 = mean_start(2, jnp.concatenate([top, low], axis=0))
     pending += mean1
-    middle1 = mean_middle(1, mean1)
+    middle1 = mean_middle(2, mean1)
     pending += middle1
-    gram = mean_end(1, middle1)
+    gram = mean_end(2, middle1)
     qq, pw, alpha2, ww = gram[:k, :k], gram[:k, k:], gram[k:, :k], gram[k:, k:]
     rest = pw - dot(qq, alpha2)
     beta2, inv2 = factor(ww - dot(pw, alpha2, TN) - dot(alpha2, rest, TN))
     out = dot(inv2, w2 - dot(alpha2, v2, TN))
     for p in range(piece):
-        next_ref[p] = out[:, p * orb : (p + 1) * orb]
-    alphas_ref[0] = alpha1
-    alphas_ref[1] = alpha2
-    betas_ref[0] = beta1
-    betas_ref[1] = beta2
+        packed_ref[p, :, :orb] = out[:, p * orb : (p + 1) * orb]
+    packed_ref[piece, :, : 4 * k] = jnp.concatenate([alpha1, alpha2, beta1, beta2], axis=1)
     for copy in pending:
         copy.wait_send()
+
+
+def finish(packed_ref, alphas_ref, betas_ref, next_ref):
+    piece, k, _ = next_ref.shape
+    small = packed_ref[piece]
+    for step in range(2):
+        alphas_ref[step] = small[:, step * k : (step + 1) * k]
+        betas_ref[step] = small[:, (2 + step) * k : (3 + step) * k]
+    next_ref[...] = packed_ref[:piece]
 
 
 def on_device(nr, nc, start_block, blocks, slot_row, slot_col, counts):
@@ -253,19 +269,14 @@
     total = float(piece * nr * nc * orb)
     group = max(g for g in range(1, 65) if capacity % g == 0 and g * local_rows * k <= 64 * 128)
     vmem = pl.BlockSpec(memory_space=pltpu.VMEM)
-    smem = pl.BlockSpec(memory_space=pltpu.SMEM)
     dma = pltpu.SemaphoreType.DMA
     width = 4 * 2 * k
     height = 2 * k // 4
-    return pl.pallas_call(
+    packed = pl.pallas_call(
         functools.partial(kernel, nr, nc, group, total),
-        out_shape=(
-            jax.ShapeDtypeStruct((2, k, k), F32),
-            jax.ShapeDtypeStruct((2, k, k), F32),
-            jax.ShapeDtypeStruct((piece, k, orb), F32),
-        ),
-        in_specs=[smem, smem, smem, vmem, pl.BlockSpec(memory_space=pl.ANY)],
-        out_specs=(vmem, vmem, vmem),
+        out_shape=jax.ShapeDtypeStruct((piece + 1, k, orb), F32),
+        in_specs=[pl.BlockSpec(memory_space=pltpu.HBM)] * 5,
+        out_specs=vmem,
         scratch_shapes=[
             pltpu.VMEM((capacity, orb, orb), F32),
             pltpu.VMEM((capacity, 2 * orb, orb), BF16),
@@ -276,20 +287,33 @@
             pltpu.VMEM((2, nc, piece, k, orb), F32),
             pltpu.VMEM((2, nc, piece, k, orb), F32),
             pltpu.VMEM((piece, k, orb), F32),
-            pltpu.VMEM((2, height, width), F32),
-            pltpu.VMEM((2, nr, height, width), F32),
-            pltpu.VMEM((2, height, width), F32),
-            pltpu.VMEM((2, nc, height, width), F32),
-            dma,
+            pltpu.VMEM((3, height, width), F32),
+            pltpu.VMEM((3, nr, height, width), F32),
+            pltpu.VMEM((3, height, width), F32),
+            pltpu.VMEM((3, nc, height, width), F32),
+            pltpu.SMEM((capacity,), jnp.int32),
+            pltpu.SMEM((capacity,), jnp.int32),
+            pltpu.SMEM((1, 1), jnp.int32),
+            dma((5,)),
             dma((2, nr)), dma((2, nr)),
             dma((2, nc)), dma((2, nc)),
-            dma((2, nr)), dma((2, nr)),
-            dma((2, nc)), dma((2, nc)),
+            dma((3, nr)), dma((3, nr)),
+            dma((3, nc)), dma((3, nc)),
         ],
         compiler_params=pltpu.CompilerParams(
-            collective_id=0, has_side_effects=True, vmem_limit_bytes=60 * 1024 * 1024
+            collective_id=0, has_side_effects=True, vmem_limit_bytes=61 << 20
         ),
-    )(slot_row[0, 0], slot_col[0, 0], counts[0], start_block, blocks[0, 0])
+    )(slot_row[0, 0], slot_col[0, 0], counts, start_block, blocks[0, 0])
+    return pl.pallas_call(
+        finish,
+        out_shape=(
+            jax.ShapeDtypeStruct((2, k, k), F32),
+            jax.ShapeDtypeStruct((2, k, k), F32),
+            jax.ShapeDtypeStruct((piece, k, orb), F32),
+        ),
+        in_specs=[vmem],
+        out_specs=(vmem, vmem, vmem),
+    )(packed)
 
 
 def solution(mesh):

time: 45 us -> 41.5 us (0.922)
  local copies, waits for them, and re-layouts: 3.97 us -> 0 us
  Pallas kernels: 39.2 us -> 40 us
    unnamed x3 -> x0, local copies, waits for them, and re-layouts: 3.97 us -> none
    pallas_call x0 -> x1, Pallas kernels: none -> 1.43 us  [on_device(): pl.pallas_call(finish, out_shape=(jax.ShapeDtypeStruct((2, k, k), F32), j...]
    pallas_call x1, Pallas kernels: 39.2 us -> 38.6 us  [on_device(): pl.pallas_call(functools.partial(kernel, nr, nc, group, total), out_shape...]
where the time goes in v2:
time: 41.5 us; the launch traced here: 41.3 us
  Pallas kernels  40 us (96%)
  between operations  1.29 us (3%)
    pallas_call x1, Pallas kernels, on_device(): pl.pallas_call(functools.partial(kernel, nr, nc, group, total), out_shape...  38.6 us
    pallas_call x1, Pallas kernels, on_device(): pl.pallas_call(finish, out_shape=(jax.ShapeDtypeStruct((2, k, k), F32), j...  1.43 us

profile of v2, /device:TPU:0, one launch (start us, length us, event | category | flops | bytes accessed | tf_op | source)
XLA Modules:
  0.0 41.3 jit_solution(1950195056947983161)
XLA Ops:
  1.3 38.6 %shard_map.76.packed_ref = f32[3,16,128]{2,1,0:T(8,128)} custom-call(s32[58]{0:T(128)} %bitcast.4, s32[58]{0:T(128)} %bitcast.5, s32[1,1]{1,0:T(1,128)S(6)} %copy.8.counts_hbm, f32[2,16,128]{2,1,0:T(8,128)} %start_ref.1, f32[58,128,128]{2,1,0:T(8,128)} %bitcast.3), custom_call_target="tpu_custom_call" | custom-call | tf_op jit(solution)/shard_map/pallas_call | solution.py:275
  39.9 1.4 %shard_map.77 = (f32[2,16,16]{2,1,0:T(8,128)}, f32[2,16,16]{2,1,0:T(8,128)}, f32[2,16,128]{2,1,0:T(8,128)}) custom-call(f32[3,16,128]{2,1,0:T(8,128)} %shard_map.76.packed_ref), custom_call_target="tpu_custom_call" | custom-call | tf_op jit(solution)/shard_map/pallas_call | solution.py:307

commit v3 on v2

--- a/solution.py
+++ b/solution.py
@@ -120,14 +120,20 @@
         gsend[step] = pack(gram) * (1.0 / total)
         return spread_row(gsend.at[step], grow.at[step], gr_send, gr_recv, step)
 
-    def mean_middle(step, copies):
+    def mean_row(step, copies):
         received(copies)
         grow[step, pl.ds(me_r, 1)] = gsend[step][None]
         value = grow[step, 0]
         for r in range(1, nr):
             value = value + grow[step, r]
+        return value
+
+    def mean_column(step, value):
         gcol_send[step] = value
         return spread_col(gcol_send.at[step], gcol.at[step], gc_send, gc_recv, step, False)
+
+    def cat_group(step):
+        return jnp.concatenate([gat[step, r, p] for r in range(nr) for p in range(piece)], axis=1)
 
     def mean_end(step, copies):
         received(copies)
@@ -139,10 +145,6 @@
 
     loads[0].wait()
     s_cat = cat(gat[0, me_r])
-    ss = dot(s_cat, s_cat, NT)
-    ss = jnp.concatenate([ss, ss], axis=1)
-    mean_s = mean_start(0, jnp.concatenate([ss, ss], axis=0))
-    pending += mean_s
     for load in loads[1:]:
         load.wait()
     count = counts_ref[0, 0]
@@ -203,23 +205,25 @@
         return own
 
     received(first)
-    middle_s = mean_middle(0, mean_s)
+    s_all = cat_group(0)
+    ss = dot(s_all, s_all, NT)
+    ss = jnp.concatenate([ss, ss], axis=1)
+    middle_s = mean_column(0, pack(jnp.concatenate([ss, ss], axis=0)) * (1.0 / total))
     pending += middle_s
     scatter0 = operate(0)
     pending += scatter0
     _, inv0 = factor(mean_end(0, middle_s)[:k, :k])
     v1 = dot(inv0, s_cat)
+    v1_all = dot(inv0, cat_group(0))
     y_raw = reduced(0, scatter0)
     ybuf[...] = y_raw
     gat[1, pl.ds(me_r, 1)] = y_raw[None]
     second = spread_row(ybuf, gat.at[1], row_send, row_recv, 1)
     pending += second
     hv1 = dot(inv0, cat(y_raw))
-    both = jnp.concatenate([v1, hv1], axis=0)
-    mean0 = mean_start(1, dot(both, both, NT))
-    pending += mean0
     received(second)
-    middle0 = mean_middle(1, mean0)
+    both = jnp.concatenate([v1_all, dot(inv0, cat_group(1))], axis=0)
+    middle0 = mean_column(1, pack(dot(both, both, NT)) * (1.0 / total))
     pending += middle0
     scatter1 = operate(1)
     pending += scatter1
@@ -236,9 +240,9 @@
     grams = dot(both, jnp.concatenate([both, y2], axis=0), NT)
     top = grams[:k, : 2 * k]
     low = jnp.concatenate([grams[:k, 2 * k :], grams[k:, k : 2 * k]], axis=1)
-    mean1 = mean_start(2, jnp.concatenate([top, low], axis=0))
+    mean1 = mean_start(0, jnp.concatenate([top, low], axis=0))
     pending += mean1
-    middle1 = mean_middle(2, mean1)
+    middle1 = mean_column(2, mean_row(0, mean1))
     pending += middle1
     gram = mean_end(2, middle1)
     qq, pw, alpha2, ww = gram[:k, :k], gram[:k, k:], gram[k:, :k], gram[k:, k:]
@@ -287,8 +291,8 @@
             pltpu.VMEM((2, nc, piece, k, orb), F32),
             pltpu.VMEM((2, nc, piece, k, orb), F32),
             pltpu.VMEM((piece, k, orb), F32),
-            pltpu.VMEM((3, height, width), F32),
-            pltpu.VMEM((3, nr, height, width), F32),
+            pltpu.VMEM((1, height, width), F32),
+            pltpu.VMEM((1, nr, height, width), F32),
             pltpu.VMEM((3, height, width), F32),
             pltpu.VMEM((3, nc, height, width), F32),
             pltpu.SMEM((capacity,), jnp.int32),
@@ -297,7 +301,7 @@
             dma((5,)),
             dma((2, nr)), dma((2, nr)),
             dma((2, nc)), dma((2, nc)),
-            dma((3, nr)), dma((3, nr)),
+            dma((1, nr)), dma((1, nr)),
             dma((3, nc)), dma((3, nc)),
         ],
         compiler_params=pltpu.CompilerParams(

time: 41.5 us -> 41 us (0.988)
  Pallas kernels: 40 us -> 39.5 us
    pallas_call x1, Pallas kernels: 38.6 us -> 38.1 us  [on_device(): pl.pallas_call(functools.partial(kernel, nr, nc, group, total), out_shape...]
where the time goes in v3:
time: 41 us; the launch traced here: 40.8 us
  Pallas kernels  39.5 us (96%)
  between operations  1.29 us (3%)
    pallas_call x1, Pallas kernels, on_device(): pl.pallas_call(functools.partial(kernel, nr, nc, group, total), out_shape...  38.1 us
    pallas_call x1, Pallas kernels, on_device(): pl.pallas_call(finish, out_shape=(jax.ShapeDtypeStruct((2, k, k), F32), j...  1.43 us

profile of v3, /device:TPU:0, one launch (start us, length us, event | category | flops | bytes accessed | tf_op | source)
XLA Modules:
  0.0 40.8 jit_solution(2051687379414460784)
XLA Ops:
  1.3 38.1 %shard_map.76.packed_ref = f32[3,16,128]{2,1,0:T(8,128)} custom-call(s32[58]{0:T(128)} %bitcast.4, s32[58]{0:T(128)} %bitcast.5, s32[1,1]{1,0:T(1,128)S(6)} %copy.8.counts_hbm, f32[2,16,128]{2,1,0:T(8,128)} %start_ref.1, f32[58,128,128]{2,1,0:T(8,128)} %bitcast.3), custom_call_target="tpu_custom_call" | custom-call | tf_op jit(solution)/shard_map/pallas_call | solution.py:279
  39.4 1.4 %shard_map.77 = (f32[2,16,16]{2,1,0:T(8,128)}, f32[2,16,16]{2,1,0:T(8,128)}, f32[2,16,128]{2,1,0:T(8,128)}) custom-call(f32[3,16,128]{2,1,0:T(8,128)} %shard_map.76.packed_ref), custom_call_target="tpu_custom_call" | custom-call | tf_op jit(solution)/shard_map/pallas_call | solution.py:311
